TPU v7x, 32 devices: a whole 2x2x4 slice. The times are simulated.
32 devices in a mesh: row: 8 (over y, x, core), col: 4 (over z).
Axes of the slice: x: 2, y: 2, z: 4, core: 2. Of those that a mesh axis runs over, the one named last changes fastest.
Arguments:
- block_input: bfloat16 [8192, 768], P(('row', 'col'))
- block_cotangent: bfloat16 [8192, 768], P(('row', 'col')), may hold values from -6 to 6
- block_lengths: int32 [64], P(('row', 'col')), may hold values from 1 to 128, as said below
- block_offsets: int32 [64], P(('row', 'col')), may hold values from 0 to 128, as said below
- norm1_gain: float32 [768], replicated, may hold values from 0.25 to 1.75
- norm1_bias: float32 [768], replicated, may hold values from -2.5 to 2.5
- norm2_gain: float32 [768], replicated, may hold values from 0.25 to 1.75
- norm2_bias: float32 [768], replicated, may hold values from -2.5 to 2.5
- qkv_weight: bfloat16 [768, 2304], P('row', 'col'), may hold values from -0.21875 to 0.21875
- qkv_bias: float32 [2304], P('col'), may hold values from -3 to 3
- dense_weight: bfloat16 [768, 768], P('col', 'row'), may hold values from -0.875 to 0.875
- dense_bias: float32 [768], replicated, may hold values from -2.5 to 2.5
- fc_in_weight: bfloat16 [768, 3072], P('row', 'col'), may hold values from -0.21875 to 0.21875
- fc_in_bias: float32 [3072], P('col'), may hold values from -3 to 3
- fc_out_weight: bfloat16 [3072, 768], P('col', 'row'), may hold values from -0.109375 to 0.109375
- fc_out_bias: float32 [768], replicated, may hold values from -2.5 to 2.5
Outputs:
- block_out: float32 [8192, 768], P(('row', 'col'))
- input_grad: float32 [8192, 768], P(('row', 'col'))
- norm1_gain_grad: float32 [768], replicated
- norm1_bias_grad: float32 [768], replicated
- norm2_gain_grad: float32 [768], replicated
- norm2_bias_grad: float32 [768], replicated
- qkv_weight_grad: float32 [768, 2304], P('row', 'col')
- qkv_bias_grad: float32 [2304], P('col')
- dense_weight_grad: float32 [768, 768], P('col', 'row')
- dense_bias_grad: float32 [768], replicated
- fc_in_weight_grad: float32 [768, 3072], P('row', 'col')
- fc_in_bias_grad: float32 [3072], P('col')
- fc_out_weight_grad: float32 [3072, 768], P('col', 'row')
- fc_out_bias_grad: float32 [768], replicated
Inputs may be any that keep to these rules, and one draw needn't show every extreme that they name: `block_lengths`: blocks come in aligned pairs. A pair holds either two sequences, each in its own block, or one sequence over both blocks, whose first block is then full. `block_offsets`: an even block's offset is 0; an odd block's is 0 when it starts a sequence and 128 when it continues the sequence of the block before it.
All inputs are finite; a program needn't handle non-finite values.
Results may differ from a plain program's by a relative error of at most 0.0088.
Values may be sent and summed in bfloat16 or wider, within the bound.
A program may use at most 128 MiB of HBM per device.

v0:
```python
import math
import jax
import jax.numpy as jnp
from jax import lax
from jax.sharding import PartitionSpec as P

HEADS = 12
ROT = 16
NORM_EPSILON = 1e-05
HALF_ROOT = math.sqrt(0.5)
DENSITY_SCALE = 1.0 / math.sqrt(2.0 * math.pi)


def normalize(features):
    widened = features.astype(jnp.float32)
    centered = widened - jnp.mean(widened, axis=1, keepdims=True)
    inverse = lax.rsqrt(jnp.mean(centered * centered, axis=1, keepdims=True) + NORM_EPSILON)
    return (centered * inverse, inverse)


def norm_back(grad_normed, gain, standard, inverse):
    grad_unit = grad_normed * gain
    return inverse * (
        grad_unit
        - jnp.mean(grad_unit, axis=1, keepdims=True)
        - standard * jnp.mean(grad_unit * standard, axis=1, keepdims=True)
    )


def gelu_exact(pre_act):
    return 0.5 * pre_act * (1.0 + lax.erf(pre_act * HALF_ROOT))


def gelu_slope(pre_act):
    return (
        0.5 * (1.0 + lax.erf(pre_act * HALF_ROOT))
        + pre_act * jnp.exp(-0.5 * pre_act * pre_act) * DENSITY_SCALE
    )


def rotary_tables(positions, rotated):
    halves = rotated // 2
    frequency = 10000.0 ** (-2.0 * jnp.arange(halves, dtype=jnp.float32) / rotated)
    angles = positions[:, None].astype(jnp.float32) * frequency[None, :]
    angles = jnp.concatenate([angles, angles], axis=1)
    return (jnp.cos(angles)[:, None, :], jnp.sin(angles)[:, None, :])


def rotate(values, cosine, sine_table, rotated):
    halves = rotated // 2
    leading = values[..., :rotated]
    turned = jnp.concatenate([-leading[..., halves:], leading[..., :halves]], axis=-1)
    return jnp.concatenate([leading * cosine + turned * sine_table, values[..., rotated:]], axis=-1)


def unrotate(gradient, cosine, sine_table, rotated):
    halves = rotated // 2
    leading = gradient[..., :rotated]
    scaled = leading * sine_table
    turned = jnp.concatenate([scaled[..., halves:], -scaled[..., :halves]], axis=-1)
    return jnp.concatenate([leading * cosine + turned, gradient[..., rotated:]], axis=-1)


def pair_mask(lengths, offsets, block_rows):
    pair_count = lengths.shape[0] // 2
    local_rows = jnp.arange(2 * block_rows, dtype=jnp.int32)
    block_of = local_rows // block_rows
    in_block = local_rows % block_rows
    pair_lengths = lengths.reshape(pair_count, 2)
    joined = offsets.reshape(pair_count, 2)[:, 1] > 0
    row_limit = jnp.where(block_of[None, :] == 0, pair_lengths[:, 0:1], pair_lengths[:, 1:2])
    live_keys = in_block[None, :] < row_limit
    same_seq = (block_of[:, None] == block_of[None, :])[None, :, :] | joined[:, None, None]
    causal = (local_rows[None, :] <= local_rows[:, None])[None, :, :]
    diagonal = (local_rows[:, None] == local_rows[None, :])[None, :, :]
    return same_seq & causal & (live_keys[:, None, :] | diagonal)


def masked_scores(queries, key_rows, allowed, score_scale):
    scores = (
        jnp.einsum("pihd,pjhd->phij", queries, key_rows, preferred_element_type=jnp.float32)
        * score_scale
    )
    return jnp.where(allowed[:, None, :, :], scores, -jnp.inf)


def on_device(
    block_input,
    block_cotangent,
    block_lengths,
    block_offsets,
    norm1_gain,
    norm1_bias,
    norm2_gain,
    norm2_bias,
    qkv_weight,
    qkv_bias,
    dense_weight,
    dense_bias,
    fc_in_weight,
    fc_in_bias,
    fc_out_weight,
    fc_out_bias,
):
    groups = lax.axis_size("col")
    col_index = lax.axis_index("col")
    own_rows = block_input.shape[0]
    width = block_input.shape[1]
    head_dim = width // HEADS
    block_count = block_lengths.shape[0]
    block_rows = own_rows // block_count
    pair_count = block_count // 2
    four_shape = (pair_count, 2 * block_rows, HEADS, head_dim)
    score_scale = head_dim ** (-0.5)
    contract_rows = (((0,), (0,)), ((), ()))
    in_block = jnp.arange(block_rows, dtype=jnp.int32)
    positions = (block_offsets[:, None] + in_block[None, :]).reshape(-1)
    valid = (in_block[None, :] < block_lengths[:, None]).reshape(-1)
    cosine, sine_table = rotary_tables(positions, ROT)
    allowed = pair_mask(block_lengths, block_offsets, block_rows)
    standard, inverse = normalize(block_input)
    normed_first = (standard * norm1_gain + norm1_bias).astype(jnp.bfloat16)
    normed_second = (standard * norm2_gain + norm2_bias).astype(jnp.bfloat16)
    first_rows, second_rows = (
        lax.all_gather(normed_first, "col", axis=0, tiled=True),
        lax.all_gather(normed_second, "col", axis=0, tiled=True),
    )
    qkv_block, fc_in_block, dense_block, fc_out_block = (
        lax.all_gather(qkv_weight, "row", axis=0, tiled=True),
        lax.all_gather(fc_in_weight, "row", axis=0, tiled=True),
        lax.all_gather(dense_weight, "row", axis=1, tiled=True),
        lax.all_gather(fc_out_weight, "row", axis=1, tiled=True),
    )
    mixed_rows = (
        jnp.dot(first_rows, qkv_block, preferred_element_type=jnp.float32) + qkv_bias
    ).astype(jnp.bfloat16)
    mixed_own = lax.all_to_all(mixed_rows, "col", split_axis=0, concat_axis=1, tiled=True)
    mixed_own = mixed_own.reshape(own_rows, 3, HEADS, head_dim)
    queries = rotate(mixed_own[:, 0].astype(jnp.float32), cosine, sine_table, ROT).astype(
        jnp.bfloat16
    )
    key_rows = rotate(mixed_own[:, 1].astype(jnp.float32), cosine, sine_table, ROT).astype(
        jnp.bfloat16
    )
    queries = queries.reshape(four_shape)
    key_rows = key_rows.reshape(four_shape)
    values = mixed_own[:, 2].reshape(four_shape)
    scores = masked_scores(queries, key_rows, allowed, score_scale)
    highest = jnp.max(scores, axis=-1, keepdims=True)
    totals = highest + jnp.log(jnp.sum(jnp.exp(scores - highest), axis=-1, keepdims=True))
    weights = jnp.exp(scores - totals).astype(jnp.bfloat16)
    attended = jnp.einsum("phij,pjhd->pihd", weights, values, preferred_element_type=jnp.float32)
    attended = attended.astype(jnp.bfloat16).reshape(own_rows, width)
    attended_rows = lax.all_to_all(attended, "col", split_axis=1, concat_axis=0, tiled=True)
    pre_act = jnp.dot(second_rows, fc_in_block, preferred_element_type=jnp.float32) + fc_in_bias
    hidden = gelu_exact(pre_act).astype(jnp.bfloat16)
    summed = lax.psum_scatter(
        (
            jnp.dot(attended_rows, dense_block, preferred_element_type=jnp.float32)
            + jnp.dot(hidden, fc_out_block, preferred_element_type=jnp.float32)
        ).astype(jnp.bfloat16),
        "col",
        scatter_dimension=0,
        tiled=True,
    ).astype(jnp.float32)
    block_out = block_input.astype(jnp.float32) + dense_bias + fc_out_bias + summed
    grad_out = jnp.where(valid[:, None], block_cotangent, jnp.zeros_like(block_cotangent))
    grad_rows = lax.all_gather(grad_out, "col", axis=0, tiled=True)
    grad_hidden = jnp.dot(grad_rows, fc_out_block.T, preferred_element_type=jnp.float32)
    grad_pre = (grad_hidden * gelu_slope(pre_act)).astype(jnp.bfloat16)
    grad_att_rows = jnp.dot(grad_rows, dense_block.T, preferred_element_type=jnp.float32).astype(
        jnp.bfloat16
    )
    grad_att = lax.all_to_all(
        grad_att_rows, "col", split_axis=0, concat_axis=1, tiled=True
    ).reshape(four_shape)
    probability = jnp.exp(scores - totals)
    grad_probs = jnp.einsum("pihd,pjhd->phij", grad_att, values, preferred_element_type=jnp.float32)
    row_dot = jnp.sum(probability * grad_probs, axis=-1, keepdims=True)
    grad_scores = (probability * (grad_probs - row_dot) * score_scale).astype(jnp.bfloat16)
    grad_query = jnp.einsum(
        "phij,pjhd->pihd", grad_scores, key_rows, preferred_element_type=jnp.float32
    )
    grad_key = jnp.einsum(
        "phij,pihd->pjhd", grad_scores, queries, preferred_element_type=jnp.float32
    )
    grad_values = jnp.einsum(
        "phij,pihd->pjhd", weights, grad_att, preferred_element_type=jnp.float32
    )
    grad_query = unrotate(
        grad_query.reshape(own_rows, HEADS, head_dim), cosine, sine_table, ROT
    ).astype(jnp.bfloat16)
    grad_key = unrotate(
        grad_key.reshape(own_rows, HEADS, head_dim), cosine, sine_table, ROT
    ).astype(jnp.bfloat16)
    grad_values = grad_values.astype(jnp.bfloat16).reshape(own_rows, HEADS, head_dim)
    grad_mixed = jnp.stack([grad_query, grad_key, grad_values], axis=1).reshape(own_rows, 3 * width)
    grad_mixed_rows = lax.all_to_all(grad_mixed, "col", split_axis=1, concat_axis=0, tiled=True)
    grad_qkv_w = lax.dot_general(
        first_rows, grad_mixed_rows, contract_rows, preferred_element_type=jnp.float32
    )
    grad_in_w = lax.dot_general(
        second_rows, grad_pre, contract_rows, preferred_element_type=jnp.float32
    )
    qkv_weight_grad, fc_in_weight_grad = (
        lax.psum_scatter(grad_qkv_w, "row", scatter_dimension=0, tiled=True),
        lax.psum_scatter(grad_in_w, "row", scatter_dimension=0, tiled=True),
    )
    grad_dense_w = lax.dot_general(
        attended_rows, grad_rows, contract_rows, preferred_element_type=jnp.float32
    )
    grad_out_w = lax.dot_general(
        hidden, grad_rows, contract_rows, preferred_element_type=jnp.float32
    )
    dense_weight_grad, fc_out_weight_grad = (
        lax.psum_scatter(grad_dense_w, "row", scatter_dimension=1, tiled=True),
        lax.psum_scatter(grad_out_w, "row", scatter_dimension=1, tiled=True),
    )
    back_first_rows = jnp.dot(grad_mixed_rows, qkv_block.T, preferred_element_type=jnp.float32)
    back_second_rows = jnp.dot(grad_pre, fc_in_block.T, preferred_element_type=jnp.float32)
    back_first, back_second = (
        lax.psum_scatter(back_first_rows, "col", scatter_dimension=0, tiled=True),
        lax.psum_scatter(back_second_rows, "col", scatter_dimension=0, tiled=True),
    )
    input_grad = (
        grad_out.astype(jnp.float32)
        + norm_back(back_first, norm1_gain, standard, inverse)
        + norm_back(back_second, norm2_gain, standard, inverse)
    )
    norm_sums = (
        jnp.sum(back_first * standard, axis=0),
        jnp.sum(back_first, axis=0),
        jnp.sum(back_second * standard, axis=0),
        jnp.sum(back_second, axis=0),
    )
    qkv_cols = grad_mixed_rows.shape[1]
    ff_cols = grad_pre.shape[1]
    column_mask = (jnp.arange(groups, dtype=jnp.int32) == col_index)[:, None]
    qkv_bias_part = jnp.sum(grad_mixed_rows, axis=0, dtype=jnp.float32)
    in_bias_part = jnp.sum(grad_pre, axis=0, dtype=jnp.float32)
    spread_qkv = jnp.where(column_mask, qkv_bias_part[None, :], 0.0).reshape(-1)
    spread_in = jnp.where(column_mask, in_bias_part[None, :], 0.0).reshape(-1)
    gain_one, bias_one, gain_two, bias_two, out_bias, total_qkv, total_in = lax.psum(
        (
            norm_sums[0],
            norm_sums[1],
            norm_sums[2],
            norm_sums[3],
            jnp.sum(grad_out, axis=0, dtype=jnp.float32),
            spread_qkv,
            spread_in,
        ),
        ("row", "col"),
    )
    qkv_bias_grad = lax.dynamic_slice_in_dim(total_qkv, col_index * qkv_cols, qkv_cols, 0)
    fc_in_bias_grad = lax.dynamic_slice_in_dim(total_in, col_index * ff_cols, ff_cols, 0)
    return (
        block_out,
        input_grad,
        gain_one,
        bias_one,
        gain_two,
        bias_two,
        qkv_weight_grad,
        qkv_bias_grad,
        dense_weight_grad,
        out_bias,
        fc_in_weight_grad,
        fc_in_bias_grad,
        fc_out_weight_grad,
        out_bias,
    )


def solution(mesh):
    return jax.shard_map(
        on_device,
        mesh=mesh,
        in_specs=(
            P(("row", "col"), None),
            P(("row", "col"), None),
            P(("row", "col")),
            P(("row", "col")),
            P(),
            P(),
            P(),
            P(),
            P("row", "col"),
            P("col"),
            P("col", "row"),
            P(),
            P("row", "col"),
            P("col"),
            P("col", "row"),
            P(),
        ),
        out_specs=(
            P(("row", "col"), None),
            P(("row", "col"), None),
            P(),
            P(),
            P(),
            P(),
            P("row", "col"),
            P("col"),
            P("col", "row"),
            P(),
            P("row", "col"),
            P("col"),
            P("col", "row"),
            P(),
        ),
        check_vma=False,
    )
```

profile of v0, /device:TPU:0, one launch (start us, length us, event | category | flops | bytes accessed | tf_op | source)
XLA Modules:
  0.0 555.2 jit_solution(1927547153196983552)
XLA Ops:
  9.7 2.2 fusion.38
  15.7 12.3 %all_gather.22 = bf16[768,576]{1,0:T(8,128)(2,1)S(1)} all-gather(bf16[96,576]{1,0:T(8,128)(2,1)S(1)} %copy-done.18), channel_id=1, replica_groups=mesh['row'=8,'col'=4] {'row'}, dimensions={0}, use_global_device_ids=true | all-gather | bytes 995328 | tf_op jit(solution)/shard_map/all_gather | solution.py:129
  28.0 23.8 %all-gather.6.cloned.1.call-done = bf16[1024,768]{1,0:T(8,128)(2,1)} async-done(((bf16[256,768]{1,0:T(8,128)(2,1)}), bf16[1024,768]{1,0:T(8,128)(2,1)}) %all-gather.6.cloned.1.call-update) | async-done | bytes 1572880 | tf_op jit(solution)/shard_map/all_gather | solution.py:125
  51.8 2.5 add_convert_fusion.1
  55.5 3.5 all-to-all-start
  63.2 23.8 %all-to-all-done = bf16[4,256,576]{1,2,0:T(8,128)(2,1)S(1)} async-done(((bf16[4,256,576]{1,2,0:T(8,128)(2,1)}), bf16[4,256,576]{1,2,0:T(8,128)(2,1)S(1)}, u32[]{:S(2)}, u32[]{:S(2)}) %all-to-all-start) | async-done | bytes 1179680 | tf_op jit(solution)/shard_map/all_to_all | solution.py:137
  91.2 3.5 all-to-all-start.1
  94.7 29.5 %all-gather.8.cloned.1.call-done = bf16[1024,768]{1,0:T(8,128)(2,1)} async-done(((bf16[256,768]{1,0:T(8,128)(2,1)}), bf16[1024,768]{1,0:T(8,128)(2,1)}) %all-gather.8.cloned.1.call-update) | async-done | bytes 1572880 | tf_op jit(solution)/shard_map/all_gather | solution.py:126
  124.2 5.4 multiply_convert_fusion.1
  129.6 31.8 %all-gather.14.cloned.1.call-done = bf16[1024,768]{1,0:T(8,128)(2,1)} async-done(((bf16[256,768]{1,0:T(8,128)(2,1)}), bf16[1024,768]{1,0:T(8,128)(2,1)}) %all-gather.14.cloned.1.call-update) | async-done | bytes 1572880 | tf_op jit(solution)/shard_map/all_gather | solution.py:168
  161.4 3.1 convolution_bitcast_fusion
  164.6 21.3 %all-gather.12.cloned.1.call-done = bf16[768,768]{0,1:T(8,128)(2,1)} async-done(((bf16[768,96]{0,1:T(8,128)(2,1)}), bf16[768,768]{0,1:T(8,128)(2,1)}) %all-gather.12.cloned.1.call-update) | async-done | bytes 1179664 | tf_op jit(solution)/shard_map/all_gather | solution.py:132
  186.0 4.7 convert_reduce_fusion
  191.9 3.1 fusion.99
  196.5 9.5 %all_gather.23 = bf16[192,768]{0,1:T(8,128)(2,1)S(1)} all-gather(bf16[192,96]{0,1:T(8,128)(2,1)} %copy.47), channel_id=1, replica_groups=mesh['row'=8,'col'=4] {'row'}, dimensions={1}, use_global_device_ids=true | all-gather | bytes 331776 | tf_op jit(solution)/shard_map/all_gather | solution.py:131
  206.7 16.6 %all_to_all.70 = bf16[4,256,192]{1,2,0:T(8,128)(2,1)S(1)} all-to-all(bf16[4,256,192]{1,2,0:T(8,128)(2,1)S(1)} %bitcast.111), channel_id=1, replica_groups=mesh['row'=8,'col'=4] {'col'}, dimensions={0} | all-to-all | bytes 786432 | tf_op jit(solution)/shard_map/all_to_all | solution.py:174
  224.1 2.3 fusion.53
  226.4 7.0 %fusion.19 = f32[256,12,64]{0,2,1:T(8,128)S(1)} fusion(f32[12,256,256]{1,2,0:T(8,128)} %fusion.53, f32[12,256,256]{1,2,0:T(8,128)} %copy-done.3, f32[12,256]{1,0:T(8,128)} %copy-done.29, pred[256,256]{0,1:T(8,128)(4,1)} %copy-done.14, bf16[256,12,48]{0,2,1:T(8,128)(2,1)} %copy-done.11, bf16[256,12,16]{0,2,1:T(8,128)(2,1)} %copy-done.20), kind=kOutput, calls=%fused_computation.25 | convolution fusion | flops 110103808 | bytes 7548928 | tf_op jit(solution)/shard_map/phij,pjhd->pihd/dot_general | solution.py:181
  233.4 7.8 %fusion.22 = f32[256,12,64]{0,2,1:T(8,128)} fusion(f32[12,256,256]{1,2,0:T(8,128)} %fusion.53, f32[12,256,256]{1,2,0:T(8,128)} %copy-done.3, f32[12,256]{1,0:T(8,128)S(1)} %copy-done.30, pred[256,256]{0,1:T(8,128)(4,1)} %copy-done.14, bf16[256,12,48]{0,2,1:T(8,128)(2,1)S(1)} %copy-done.13, bf16[256,12,16]{0,2,1:T(8,128)(2,1)} %copy-done.19), kind=kOutput, calls=%fused_computation.26 | convolution fusion | flops 110103808 | bytes 7548928 | tf_op jit(solution)/shard_map/phij,pihd->pjhd/dot_general | solution.py:184
  245.6 61.8 %all_to_all.71 = bf16[256,4,576]{0,2,1:T(8,128)(2,1)S(1)} all-to-all(bf16[256,4,576]{0,2,1:T(8,128)(2,1)S(1)} %bitcast.104), channel_id=1, replica_groups=mesh['row'=8,'col'=4] {'col'}, dimensions={1} | all-to-all | bytes 2359296 | tf_op jit(solution)/shard_map/all_to_all | solution.py:198
  308.6 3.2 fusion.98
  311.8 3.2 fusion.97
  316.9 4.8 fusion.101
  321.7 4.3 fusion.102
  326.4 4.6 fusion.100
  333.4 40.4 %reduce-scatter.12.cloned.1.call-done = f32[256,768]{1,0:T(8,128)} async-done(((f32[1024,768]{1,0:T(8,128)}), f32[256,768]{1,0:T(8,128)}) %reduce-scatter.12.cloned.1.call-update) | async-done | bytes 786448 | tf_op jit(solution)/shard_map/reduce_scatter | solution.py:222
  373.8 2.1 fusion.48
  375.8 43.6 %all-reduce = (f32[768]{0:T(1024)}, f32[768]{0:T(1024)}, f32[768]{0:T(1024)}, f32[768]{0:T(1024)}, f32[2304]{0:T(1024)S(1)}, /*index=5*/f32[768]{0:T(1024)S(1)}, f32[3072]{0:T(1024)S(1)}) all-reduce(f32[768]{0:T(1024)S(1)} %get-tuple-element.16, f32[768]{0:T(1024)S(1)} %get-tuple-element.21, ...), channel_id=1, replica_groups=mesh['row'=8,'col'=4] {'row','col'}, use_global_device_ids=true, to_apply=%region_13.14 | all-reduce | flops 9216 | bytes 73728 | tf_op jit(solution)/shard_map/psum | solution.py:243
  420.9 3.2 fusion.47
  424.1 33.4 %reduce-scatter.18.cloned.1.call-done = f32[96,768]{1,0:T(8,128)} async-done(((f32[768,768]{1,0:T(8,128)}), f32[96,768]{1,0:T(8,128)}) %reduce-scatter.18.cloned.1.call-update) | async-done | bytes 294928 | tf_op jit(solution)/shard_map/reduce_scatter | solution.py:207
  457.5 46.3 %reduce-scatter.20.cloned.1.call-done = f32[768,96]{0,1:T(8,128)} async-done(((f32[768,768]{0,1:T(8,128)}), f32[768,96]{0,1:T(8,128)}) %reduce-scatter.20.cloned.1.call-update) | async-done | bytes 294928 | tf_op jit(solution)/shard_map/reduce_scatter | solution.py:217
  503.8 44.0 %reduce-scatter.16.cloned.1.call-done = f32[96,576]{1,0:T(8,128)} async-done(((f32[768,576]{1,0:T(8,128)}), f32[96,576]{1,0:T(8,128)}) %reduce-scatter.16.cloned.1.call-update) | async-done | bytes 221200 | tf_op jit(solution)/shard_map/reduce_scatter | solution.py:206
  (166 shorter events, 31.1 us)
Async XLA Ops:
  7.2 8.5 %copy-start.18 = (bf16[96,576]{1,0:T(8,128)(2,1)S(1)}, bf16[96,576]{1,0:T(8,128)(2,1)}, u32[]{:S(2)}) copy-start(bf16[96,576]{1,0:T(8,128)(2,1)} %param.24) | copy-start | bytes 331780
  7.2 44.6 %copy-start.38 = (f32[576]{0:T(1024)S(1)}, f32[576]{0:T(1024)}, u32[]{:S(2)}) copy-start(f32[576]{0:T(1024)} %param.25) | copy-start | bytes 6916
  7.2 44.6 %all-gather.6.cloned.1.call-start = ((), (), s32[]{:S(2)}) async-start(), calls=%async_computation.11 | async-start | bytes 1966080 | tf_op jit(solution)/shard_map/all_gather | solution.py:125
  11.9 82.8 %all-gather.10.cloned.1.call-start = ((), (), s32[]{:S(2)}) async-start(), calls=%async_computation.13 | async-start | bytes 1327104 | tf_op jit(solution)/shard_map/all_gather | solution.py:130
  12.7 111.5 %all-gather.8.cloned.1.call-start = ((), (), s32[]{:S(2)}) async-start(), calls=%async_computation.12 | async-start | bytes 1966080 | tf_op jit(solution)/shard_map/all_gather | solution.py:126
  13.4 148.0 %all-gather.14.cloned.1.call-start = ((), (), s32[]{:S(2)}) async-start(), calls=%async_computation.16 | async-start | bytes 1966080 | tf_op jit(solution)/shard_map/all_gather | solution.py:168
  28.0 26.4 %copy-start.8 = (bf16[768,576]{1,0:T(8,128)(2,1)}, bf16[768,576]{1,0:T(8,128)(2,1)S(1)}, u32[]{:S(2)}) copy-start(bf16[768,576]{1,0:T(8,128)(2,1)S(1)} %all_gather.22) | copy-start | bytes 2654212
  55.5 31.4 %all-to-all-start = ((bf16[4,256,576]{1,2,0:T(8,128)(2,1)}), bf16[4,256,576]{1,2,0:T(8,128)(2,1)S(1)}, u32[]{:S(2)}, u32[]{:S(2)}) async-start(bf16[4,256,576]{1,2,0:T(8,128)(2,1)} %bitcast.101), calls=%async_computation | async-start | bytes 2359296 | tf_op jit(solution)/shard_map/all_to_all | solution.py:137
  59.1 126.9 %all-gather.12.cloned.1.call-start = ((), (), s32[]{:S(2)}) async-start(), calls=%async_computation.14 | async-start | bytes 1327104 | tf_op jit(solution)/shard_map/all_gather | solution.py:132
  63.0 25.8 %copy-start.16 = (f32[256,16]{0,1:T(8,128)}, f32[256,16]{0,1:T(8,128)S(1)}, u32[]{:S(2)}) copy-start(f32[256,16]{0,1:T(8,128)S(1)} %get-tuple-element.58) | copy-start | bytes 49156
  63.2 26.4 %copy-start.14 = (pred[256,256]{0,1:T(8,128)(4,1)}, pred[256,256]{0,1:T(8,128)(4,1)S(1)}, u32[]{:S(2)}) copy-start(pred[256,256]{0,1:T(8,128)(4,1)S(1)} %fusion.57) | copy-start | bytes 196612
  89.5 34.7 %copy-start.39 = (f32[768]{0:T(1024)S(1)}, f32[768]{0:T(1024)}, u32[]{:S(2)}) copy-start(f32[768]{0:T(1024)} %param.29) | copy-start | bytes 9220
  91.2 38.4 %all-to-all-start.1 = ((bf16[256,4,192]{0,2,1:T(8,128)(2,1)}), bf16[256,4,192]{0,2,1:T(8,128)(2,1)S(1)}, u32[]{:S(2)}, u32[]{:S(2)}) async-start(bf16[256,4,192]{0,2,1:T(8,128)(2,1)} %bitcast.14), calls=%async_computation.1 | async-start | bytes 786432 | tf_op jit(solution)/shard_map/all_to_all | solution.py:154
  94.6 236.6 %reduce-scatter.22.cloned.1.call-start = ((), (), s32[]{:S(2)}) async-start(), calls=%async_computation.22 | async-start | bytes 884736
  161.4 24.5 %copy-start.1 = (bf16[1024,768]{1,0:T(8,128)(2,1)S(1)}, bf16[1024,768]{1,0:T(8,128)(2,1)}, u32[]{:S(2)}) copy-start(bf16[1024,768]{1,0:T(8,128)(2,1)} %all-gather.14.cloned.1.call-done) | copy-start | bytes 4718596
  164.6 168.8 %reduce-scatter.14.cloned.1.call-start = ((), (), s32[]{:S(2)}) async-start(), calls=%async_computation.18 | async-start | bytes 3932160 | tf_op jit(solution)/shard_map/reduce_scatter | solution.py:223
  195.0 178.8 %reduce-scatter.12.cloned.1.call-start = ((), (), s32[]{:S(2)}) async-start(), calls=%async_computation.17 | async-start | bytes 3932160 | tf_op jit(solution)/shard_map/reduce_scatter | solution.py:222
  245.5 63.1 %copy-start.9 = (bf16[768,576]{1,0:T(8,128)(2,1)S(1)}, bf16[768,576]{1,0:T(8,128)(2,1)}, u32[]{:S(2)}) copy-start(bf16[768,576]{1,0:T(8,128)(2,1)} %copy-done.8) | copy-start | bytes 2654212
  311.8 109.1 %reduce-scatter.10.cloned.1.call-start = ((), (), s32[]{:S(2)}) async-start(), calls=%async_computation.15 | async-start | bytes 1966080 | tf_op jit(solution)/shard_map/reduce_scatter | solution.py:157
  316.8 140.7 %reduce-scatter.18.cloned.1.call-start = ((), (), s32[]{:S(2)}) async-start(), calls=%async_computation.20 | async-start | bytes 2654208 | tf_op jit(solution)/shard_map/reduce_scatter | solution.py:207
  321.7 182.1 %reduce-scatter.20.cloned.1.call-start = ((), (), s32[]{:S(2)}) async-start(), calls=%async_computation.21 | async-start | bytes 2654208 | tf_op jit(solution)/shard_map/reduce_scatter | solution.py:217
  326.1 221.7 %reduce-scatter.16.cloned.1.call-start = ((), (), s32[]{:S(2)}) async-start(), calls=%async_computation.19 | async-start | bytes 2211840 | tf_op jit(solution)/shard_map/reduce_scatter | solution.py:206
  331.0 42.8 %copy-start = (bf16[256,768]{1,0:T(8,128)(2,1)S(1)}, bf16[256,768]{1,0:T(8,128)(2,1)}, u32[]{:S(2)}) copy-start(bf16[256,768]{1,0:T(8,128)(2,1)} %param.16) | copy-start | bytes 1179652
  331.0 42.8 %copy-start.22 = (f32[768]{0:T(1024)S(1)}, f32[768]{0:T(1024)}, u32[]{:S(2)}) copy-start(f32[768]{0:T(1024)} %param.20) | copy-start | bytes 9220
  331.0 42.8 %copy-start.23 = (f32[768]{0:T(1024)S(1)}, f32[768]{0:T(1024)}, u32[]{:S(2)}) copy-start(f32[768]{0:T(1024)} %param.22) | copy-start | bytes 9220
  331.0 42.8 %copy-start.25 = (f32[256]{0:T(256)S(1)}, f32[256]{0:T(256)}, u32[]{:S(2)}) copy-start(f32[256]{0:T(256)} %copy-done.24) | copy-start | bytes 3076
  331.0 42.8 %copy-start.27 = (f32[256]{0:T(256)S(1)}, f32[256]{0:T(256)}, u32[]{:S(2)}) copy-start(f32[256]{0:T(256)} %copy-done.26) | copy-start | bytes 3076
  331.0 44.8 %copy-start.28 = (f32[768]{0:T(1024)S(1)}, f32[768]{0:T(1024)}, u32[]{:S(2)}) copy-start(f32[768]{0:T(1024)} %get-tuple-element.33) | copy-start | bytes 9220
  331.0 89.9 %copy-start.2 = (bf16[256,768]{1,0:T(8,128)(2,1)S(1)}, bf16[256,768]{1,0:T(8,128)(2,1)}, u32[]{:S(2)}) copy-start(bf16[256,768]{1,0:T(8,128)(2,1)} %get-tuple-element.34) | copy-start | bytes 1179652
  331.0 89.9 %copy-start.32 = (f32[768]{0:T(1024)S(1)}, f32[768]{0:T(1024)}, u32[]{:S(2)}) copy-start(f32[768]{0:T(1024)} %param.31) | copy-start | bytes 9220
  331.0 89.9 %copy-start.33 = (f32[768]{0:T(1024)S(1)}, f32[768]{0:T(1024)}, u32[]{:S(2)}) copy-start(f32[768]{0:T(1024)} %param.27) | copy-start | bytes 9220
  419.5 128.9 %copy-start.34 = (f32[768]{0:T(1024)}, f32[768]{0:T(1024)S(1)}, u32[]{:S(2)}) copy-start(f32[768]{0:T(1024)S(1)} %get-tuple-element.96) | copy-start | bytes 9220
  (24 other events, 92.4 us)
Sparse Core Ops, SparseCore 0:
  12.1 39.7 all-gather.5
  53.7 22.7 all-gather.9
  78.7 45.4 all-gather.7
  125.6 35.8 all-gather.13
  163.2 22.7 all-gather.11
  189.6 34.9 reduce-scatter.21
  226.8 79.1 reduce-scatter.13
  311.9 61.8 reduce-scatter.11
  376.0 36.3 reduce-scatter.9
  416.2 41.1 reduce-scatter.17
  461.4 42.3 reduce-scatter.19
  507.6 40.1 reduce-scatter.15
where the time goes:
time: 556 us; the launch traced here: 555 us
  waiting for transfers between devices  296 us (53%)
  blocking collectives  144 us (26%)
  matrix products  61.7 us (11%)
  other arithmetic  17.4 us (3%)
  between operations  15.5 us (3%)
  local copies, waits for them, and re-layouts  12.7 us (2%)
  starting transfers between devices  7.7 us (1%)
    all_to_all x1, blocking collectives, on_device(): lax.all_to_all(grad_mixed, 'col', split_axis=1, concat_axis=0, tiled=True)  61.8 us
    reduce_scatter x1, waiting for transfers between devices, on_device(): lax.psum_scatter(grad_out_w, 'row', scatter_dimension=1, tiled=True)  46.3 us
    reduce_scatter x1, waiting for transfers between devices, on_device(): lax.psum_scatter(grad_qkv_w, 'row', scatter_dimension=0, tiled=True)  44 us
    psum x1, blocking collectives, on_device(): lax.psum((norm_sums[0], norm_sums[1], norm_sums[2], norm_sums[3], jnp.sum...  43.6 us
    reduce_scatter x1, waiting for transfers between devices, on_device(): lax.psum_scatter(back_first_rows, 'col', scatter_dimension=0, tiled=True)  40.4 us
    reduce_scatter x1, waiting for transfers between devices, on_device(): lax.psum_scatter(grad_in_w, 'row', scatter_dimension=0, tiled=True)  33.4 us
    all_gather x1, waiting for transfers between devices, on_device(): grad_rows = lax.all_gather(grad_out, 'col', axis=0, tiled=True)  31.8 us
    all_gather x1, waiting for transfers between devices, on_device(): lax.all_gather(normed_second, 'col', axis=0, tiled=True)  29.5 us
  transfers between devices with their start and end apart: 14, of which 9 were waited for; matrix products, arithmetic and copies ran while one was open for 15% of the time, Pallas kernels for 0%

commit v1 on v0

--- a/solution.py
+++ b/solution.py
@@ -241,16 +241,19 @@
     spread_qkv = jnp.where(column_mask, qkv_bias_part[None, :], 0.0).reshape(-1)
     spread_in = jnp.where(column_mask, in_bias_part[None, :], 0.0).reshape(-1)
     gain_one, bias_one, gain_two, bias_two, out_bias, total_qkv, total_in = lax.psum(
-        (
-            norm_sums[0],
-            norm_sums[1],
-            norm_sums[2],
-            norm_sums[3],
-            jnp.sum(grad_out, axis=0, dtype=jnp.float32),
-            spread_qkv,
-            spread_in,
+        lax.psum(
+            (
+                norm_sums[0],
+                norm_sums[1],
+                norm_sums[2],
+                norm_sums[3],
+                jnp.sum(grad_out, axis=0, dtype=jnp.float32),
+                spread_qkv,
+                spread_in,
+            ),
+            "col",
         ),
-        ("row", "col"),
+        "row",
     )
     qkv_bias_grad = lax.dynamic_slice_in_dim(total_qkv, col_index * qkv_cols, qkv_cols, 0)
     fc_in_bias_grad = lax.dynamic_slice_in_dim(total_in, col_index * ff_cols, ff_cols, 0)

time: 556 us -> 556 us (level)
    psum x1, blocking collectives: 43.6 us -> 19.2 us  [on_device(): lax.psum((norm_sums[0], norm_sums[1], norm_sums[2], norm_sums[3], jnp.sum...]
    psum x0 -> x1, blocking collectives: none -> 23.8 us  [on_device(): lax.psum(lax.psum((norm_sums[0], norm_sums[1], norm_sums[2], norm_sums[3]...]
where the time goes in v1:
time: 556 us; the launch traced here: 555 us
  waiting for transfers between devices  297 us (53%)
  blocking collectives  143 us (26%)
  matrix products  61.5 us (11%)
  other arithmetic  17.3 us (3%)
  between operations  15.5 us (3%)
  local copies, waits for them, and re-layouts  12.7 us (2%)
  starting transfers between devices  7.7 us (1%)
    all_to_all x1, blocking collectives, on_device(): lax.all_to_all(grad_mixed, 'col', split_axis=1, concat_axis=0, tiled=True)  61.8 us
    reduce_scatter x1, waiting for transfers between devices, on_device(): lax.psum_scatter(grad_out_w, 'row', scatter_dimension=1, tiled=True)  46.3 us
    reduce_scatter x1, waiting for transfers between devices, on_device(): lax.psum_scatter(grad_qkv_w, 'row', scatter_dimension=0, tiled=True)  44 us
    reduce_scatter x1, waiting for transfers between devices, on_device(): lax.psum_scatter(back_first_rows, 'col', scatter_dimension=0, tiled=True)  40.5 us
    reduce_scatter x1, waiting for transfers between devices, on_device(): lax.psum_scatter(grad_in_w, 'row', scatter_dimension=0, tiled=True)  34 us
    all_gather x1, waiting for transfers between devices, on_device(): grad_rows = lax.all_gather(grad_out, 'col', axis=0, tiled=True)  31.8 us
    all_gather x1, waiting for transfers between devices, on_device(): lax.all_gather(normed_second, 'col', axis=0, tiled=True)  29.5 us
    all_gather x1, waiting for transfers between devices, on_device(): lax.all_gather(normed_first, 'col', axis=0, tiled=True)  23.8 us
  transfers between devices with their start and end apart: 14, of which 9 were waited for; matrix products, arithmetic and copies ran while one was open for 15% of the time, Pallas kernels for 0%

profile of v1, /device:TPU:0, one launch (start us, length us, event | category | flops | bytes accessed | tf_op | source)
XLA Modules:
  0.0 555.1 jit_solution(15045029151046150173)
XLA Ops:
  9.7 2.2 fusion.38
  15.7 12.3 %all_gather.22 = bf16[768,576]{1,0:T(8,128)(2,1)S(1)} all-gather(bf16[96,576]{1,0:T(8,128)(2,1)S(1)} %copy-done.18), channel_id=1, replica_groups=mesh['row'=8,'col'=4] {'row'}, dimensions={0}, use_global_device_ids=true | all-gather | bytes 995328 | tf_op jit(solution)/shard_map/all_gather | solution.py:129
  28.0 23.8 %all-gather.6.cloned.1.call-done = bf16[1024,768]{1,0:T(8,128)(2,1)} async-done(((bf16[256,768]{1,0:T(8,128)(2,1)}), bf16[1024,768]{1,0:T(8,128)(2,1)}) %all-gather.6.cloned.1.call-update) | async-done | bytes 1572880 | tf_op jit(solution)/shard_map/all_gather | solution.py:125
  51.8 2.5 add_convert_fusion.1
  55.5 3.5 all-to-all-start
  63.2 23.8 %all-to-all-done = bf16[4,256,576]{1,2,0:T(8,128)(2,1)S(1)} async-done(((bf16[4,256,576]{1,2,0:T(8,128)(2,1)}), bf16[4,256,576]{1,2,0:T(8,128)(2,1)S(1)}, u32[]{:S(2)}, u32[]{:S(2)}) %all-to-all-start) | async-done | bytes 1179680 | tf_op jit(solution)/shard_map/all_to_all | solution.py:137
  91.2 3.5 all-to-all-start.1
  94.7 29.5 %all-gather.8.cloned.1.call-done = bf16[1024,768]{1,0:T(8,128)(2,1)} async-done(((bf16[256,768]{1,0:T(8,128)(2,1)}), bf16[1024,768]{1,0:T(8,128)(2,1)}) %all-gather.8.cloned.1.call-update) | async-done | bytes 1572880 | tf_op jit(solution)/shard_map/all_gather | solution.py:126
  124.2 5.4 multiply_convert_fusion.1
  129.6 31.8 %all-gather.14.cloned.1.call-done = bf16[1024,768]{1,0:T(8,128)(2,1)} async-done(((bf16[256,768]{1,0:T(8,128)(2,1)}), bf16[1024,768]{1,0:T(8,128)(2,1)}) %all-gather.14.cloned.1.call-update) | async-done | bytes 1572880 | tf_op jit(solution)/shard_map/all_gather | solution.py:168
  161.4 3.1 convolution_bitcast_fusion
  164.6 21.3 %all-gather.12.cloned.1.call-done = bf16[768,768]{0,1:T(8,128)(2,1)} async-done(((bf16[768,96]{0,1:T(8,128)(2,1)}), bf16[768,768]{0,1:T(8,128)(2,1)}) %all-gather.12.cloned.1.call-update) | async-done | bytes 1179664 | tf_op jit(solution)/shard_map/all_gather | solution.py:132
  186.0 4.7 convert_reduce_fusion
  191.9 3.1 fusion.99
  196.5 9.5 %all_gather.23 = bf16[192,768]{0,1:T(8,128)(2,1)S(1)} all-gather(bf16[192,96]{0,1:T(8,128)(2,1)} %copy.47), channel_id=1, replica_groups=mesh['row'=8,'col'=4] {'row'}, dimensions={1}, use_global_device_ids=true | all-gather | bytes 331776 | tf_op jit(solution)/shard_map/all_gather | solution.py:131
  206.7 16.6 %all_to_all.70 = bf16[4,256,192]{1,2,0:T(8,128)(2,1)S(1)} all-to-all(bf16[4,256,192]{1,2,0:T(8,128)(2,1)S(1)} %bitcast.111), channel_id=1, replica_groups=mesh['row'=8,'col'=4] {'col'}, dimensions={0} | all-to-all | bytes 786432 | tf_op jit(solution)/shard_map/all_to_all | solution.py:174
  224.1 2.3 fusion.53
  226.4 6.9 %fusion.19 = f32[256,12,64]{0,2,1:T(8,128)S(1)} fusion(f32[12,256,256]{1,2,0:T(8,128)} %fusion.53, f32[12,256,256]{1,2,0:T(8,128)} %copy-done.3, f32[12,256]{1,0:T(8,128)} %copy-done.29, pred[256,256]{0,1:T(8,128)(4,1)} %copy-done.14, bf16[256,12,48]{0,2,1:T(8,128)(2,1)} %copy-done.11, bf16[256,12,16]{0,2,1:T(8,128)(2,1)} %copy-done.20), kind=kOutput, calls=%fused_computation.25 | convolution fusion | flops 110103808 | bytes 7548928 | tf_op jit(solution)/shard_map/phij,pjhd->pihd/dot_general | solution.py:181
  233.4 7.8 %fusion.22 = f32[256,12,64]{0,2,1:T(8,128)} fusion(f32[12,256,256]{1,2,0:T(8,128)} %fusion.53, f32[12,256,256]{1,2,0:T(8,128)} %copy-done.3, f32[12,256]{1,0:T(8,128)S(1)} %copy-done.30, pred[256,256]{0,1:T(8,128)(4,1)} %copy-done.14, bf16[256,12,48]{0,2,1:T(8,128)(2,1)S(1)} %copy-done.13, bf16[256,12,16]{0,2,1:T(8,128)(2,1)} %copy-done.19), kind=kOutput, calls=%fused_computation.26 | convolution fusion | flops 110103808 | bytes 7548928 | tf_op jit(solution)/shard_map/phij,pihd->pjhd/dot_general | solution.py:184
  245.5 61.8 %all_to_all.71 = bf16[256,4,576]{0,2,1:T(8,128)(2,1)S(1)} all-to-all(bf16[256,4,576]{0,2,1:T(8,128)(2,1)S(1)} %bitcast.104), channel_id=1, replica_groups=mesh['row'=8,'col'=4] {'col'}, dimensions={1} | all-to-all | bytes 2359296 | tf_op jit(solution)/shard_map/all_to_all | solution.py:198
  308.5 3.1 fusion.98
  311.7 3.2 fusion.97
  316.8 4.8 fusion.101
  321.6 4.3 fusion.102
  326.3 4.6 fusion.100
  333.3 40.5 %reduce-scatter.12.cloned.1.call-done = f32[256,768]{1,0:T(8,128)} async-done(((f32[1024,768]{1,0:T(8,128)}), f32[256,768]{1,0:T(8,128)}) %reduce-scatter.12.cloned.1.call-update) | async-done | bytes 786448 | tf_op jit(solution)/shard_map/reduce_scatter | solution.py:222
  375.9 19.2 %all-reduce.1 = (f32[768]{0:T(1024)S(1)}, f32[768]{0:T(1024)S(1)}, f32[768]{0:T(1024)S(1)}, f32[768]{0:T(1024)S(1)}, f32[2304]{0:T(1024)S(1)}, /*index=5*/f32[768]{0:T(1024)S(1)}, f32[3072]{0:T(1024)S(1)}) all-reduce(f32[768]{0:T(1024)S(1)} %get-tuple-element.16, ...), channel_id=1, replica_groups=mesh['row'=8,'col'=4] {'col'}, use_global_device_ids=true, to_apply=%region_13.14 | all-reduce | flops 9216 | bytes 73728 | tf_op jit(solution)/shard_map/psum | solution.py:244
  395.1 23.8 %all-reduce = (f32[768]{0:T(1024)}, f32[768]{0:T(1024)}, f32[768]{0:T(1024)}, f32[768]{0:T(1024)}, f32[2304]{0:T(1024)S(1)}, /*index=5*/f32[768]{0:T(1024)S(1)}, f32[3072]{0:T(1024)S(1)}) all-reduce(f32[768]{0:T(1024)S(1)} %get-tuple-element.33, f32[768]{0:T(1024)S(1)} %get-tuple-element.34, ...), channel_id=1, replica_groups=mesh['row'=8,'col'=4] {'row'}, use_global_device_ids=true, to_apply=%region_14.15 | all-reduce | flops 9216 | bytes 73728 | tf_op jit(solution)/shard_map/psum | solution.py:243
  420.3 3.1 fusion.47
  423.4 34.0 %reduce-scatter.18.cloned.1.call-done = f32[96,768]{1,0:T(8,128)} async-done(((f32[768,768]{1,0:T(8,128)}), f32[96,768]{1,0:T(8,128)}) %reduce-scatter.18.cloned.1.call-update) | async-done | bytes 294928 | tf_op jit(solution)/shard_map/reduce_scatter | solution.py:207
  457.4 46.3 %reduce-scatter.20.cloned.1.call-done = f32[768,96]{0,1:T(8,128)} async-done(((f32[768,768]{0,1:T(8,128)}), f32[768,96]{0,1:T(8,128)}) %reduce-scatter.20.cloned.1.call-update) | async-done | bytes 294928 | tf_op jit(solution)/shard_map/reduce_scatter | solution.py:217
  503.7 44.0 %reduce-scatter.16.cloned.1.call-done = f32[96,576]{1,0:T(8,128)} async-done(((f32[768,576]{1,0:T(8,128)}), f32[96,576]{1,0:T(8,128)}) %reduce-scatter.16.cloned.1.call-update) | async-done | bytes 221200 | tf_op jit(solution)/shard_map/reduce_scatter | solution.py:206
  (167 shorter events, 33.2 us)
Async XLA Ops:
  7.2 8.5 %copy-start.18 = (bf16[96,576]{1,0:T(8,128)(2,1)S(1)}, bf16[96,576]{1,0:T(8,128)(2,1)}, u32[]{:S(2)}) copy-start(bf16[96,576]{1,0:T(8,128)(2,1)} %param.24) | copy-start | bytes 331780
  7.2 44.6 %copy-start.38 = (f32[576]{0:T(1024)S(1)}, f32[576]{0:T(1024)}, u32[]{:S(2)}) copy-start(f32[576]{0:T(1024)} %param.25) | copy-start | bytes 6916
  7.2 44.6 %all-gather.6.cloned.1.call-start = ((), (), s32[]{:S(2)}) async-start(), calls=%async_computation.11 | async-start | bytes 1966080 | tf_op jit(solution)/shard_map/all_gather | solution.py:125
  11.9 82.8 %all-gather.10.cloned.1.call-start = ((), (), s32[]{:S(2)}) async-start(), calls=%async_computation.13 | async-start | bytes 1327104 | tf_op jit(solution)/shard_map/all_gather | solution.py:130
  12.7 111.5 %all-gather.8.cloned.1.call-start = ((), (), s32[]{:S(2)}) async-start(), calls=%async_computation.12 | async-start | bytes 1966080 | tf_op jit(solution)/shard_map/all_gather | solution.py:126
  13.4 148.0 %all-gather.14.cloned.1.call-start = ((), (), s32[]{:S(2)}) async-start(), calls=%async_computation.16 | async-start | bytes 1966080 | tf_op jit(solution)/shard_map/all_gather | solution.py:168
  28.0 26.4 %copy-start.8 = (bf16[768,576]{1,0:T(8,128)(2,1)}, bf16[768,576]{1,0:T(8,128)(2,1)S(1)}, u32[]{:S(2)}) copy-start(bf16[768,576]{1,0:T(8,128)(2,1)S(1)} %all_gather.22) | copy-start | bytes 2654212
  55.5 31.4 %all-to-all-start = ((bf16[4,256,576]{1,2,0:T(8,128)(2,1)}), bf16[4,256,576]{1,2,0:T(8,128)(2,1)S(1)}, u32[]{:S(2)}, u32[]{:S(2)}) async-start(bf16[4,256,576]{1,2,0:T(8,128)(2,1)} %bitcast.101), calls=%async_computation | async-start | bytes 2359296 | tf_op jit(solution)/shard_map/all_to_all | solution.py:137
  59.1 126.9 %all-gather.12.cloned.1.call-start = ((), (), s32[]{:S(2)}) async-start(), calls=%async_computation.14 | async-start | bytes 1327104 | tf_op jit(solution)/shard_map/all_gather | solution.py:132
  63.0 25.8 %copy-start.16 = (f32[256,16]{0,1:T(8,128)}, f32[256,16]{0,1:T(8,128)S(1)}, u32[]{:S(2)}) copy-start(f32[256,16]{0,1:T(8,128)S(1)} %get-tuple-element.65) | copy-start | bytes 49156
  63.2 26.4 %copy-start.14 = (pred[256,256]{0,1:T(8,128)(4,1)}, pred[256,256]{0,1:T(8,128)(4,1)S(1)}, u32[]{:S(2)}) copy-start(pred[256,256]{0,1:T(8,128)(4,1)S(1)} %fusion.57) | copy-start | bytes 196612
  89.5 34.7 %copy-start.39 = (f32[768]{0:T(1024)S(1)}, f32[768]{0:T(1024)}, u32[]{:S(2)}) copy-start(f32[768]{0:T(1024)} %param.29) | copy-start | bytes 9220
  91.2 38.4 %all-to-all-start.1 = ((bf16[256,4,192]{0,2,1:T(8,128)(2,1)}), bf16[256,4,192]{0,2,1:T(8,128)(2,1)S(1)}, u32[]{:S(2)}, u32[]{:S(2)}) async-start(bf16[256,4,192]{0,2,1:T(8,128)(2,1)} %bitcast.14), calls=%async_computation.1 | async-start | bytes 786432 | tf_op jit(solution)/shard_map/all_to_all | solution.py:154
  94.6 236.5 %reduce-scatter.22.cloned.1.call-start = ((), (), s32[]{:S(2)}) async-start(), calls=%async_computation.22 | async-start | bytes 884736
  161.4 24.5 %copy-start.1 = (bf16[1024,768]{1,0:T(8,128)(2,1)S(1)}, bf16[1024,768]{1,0:T(8,128)(2,1)}, u32[]{:S(2)}) copy-start(bf16[1024,768]{1,0:T(8,128)(2,1)} %all-gather.14.cloned.1.call-done) | copy-start | bytes 4718596
  164.6 168.7 %reduce-scatter.14.cloned.1.call-start = ((), (), s32[]{:S(2)}) async-start(), calls=%async_computation.18 | async-start | bytes 3932160 | tf_op jit(solution)/shard_map/reduce_scatter | solution.py:223
  195.0 178.8 %reduce-scatter.12.cloned.1.call-start = ((), (), s32[]{:S(2)}) async-start(), calls=%async_computation.17 | async-start | bytes 3932160 | tf_op jit(solution)/shard_map/reduce_scatter | solution.py:222
  245.4 63.1 %copy-start.9 = (bf16[768,576]{1,0:T(8,128)(2,1)S(1)}, bf16[768,576]{1,0:T(8,128)(2,1)}, u32[]{:S(2)}) copy-start(bf16[768,576]{1,0:T(8,128)(2,1)} %copy-done.8) | copy-start | bytes 2654212
  311.7 108.5 %reduce-scatter.10.cloned.1.call-start = ((), (), s32[]{:S(2)}) async-start(), calls=%async_computation.15 | async-start | bytes 1966080 | tf_op jit(solution)/shard_map/reduce_scatter | solution.py:157
  316.7 140.6 %reduce-scatter.18.cloned.1.call-start = ((), (), s32[]{:S(2)}) async-start(), calls=%async_computation.20 | async-start | bytes 2654208 | tf_op jit(solution)/shard_map/reduce_scatter | solution.py:207
  321.6 182.1 %reduce-scatter.20.cloned.1.call-start = ((), (), s32[]{:S(2)}) async-start(), calls=%async_computation.21 | async-start | bytes 2654208 | tf_op jit(solution)/shard_map/reduce_scatter | solution.py:217
  326.0 221.7 %reduce-scatter.16.cloned.1.call-start = ((), (), s32[]{:S(2)}) async-start(), calls=%async_computation.19 | async-start | bytes 2211840 | tf_op jit(solution)/shard_map/reduce_scatter | solution.py:206
  330.9 42.9 %copy-start = (bf16[256,768]{1,0:T(8,128)(2,1)S(1)}, bf16[256,768]{1,0:T(8,128)(2,1)}, u32[]{:S(2)}) copy-start(bf16[256,768]{1,0:T(8,128)(2,1)} %param.16) | copy-start | bytes 1179652
  330.9 42.9 %copy-start.22 = (f32[768]{0:T(1024)S(1)}, f32[768]{0:T(1024)}, u32[]{:S(2)}) copy-start(f32[768]{0:T(1024)} %param.20) | copy-start | bytes 9220
  330.9 42.9 %copy-start.23 = (f32[768]{0:T(1024)S(1)}, f32[768]{0:T(1024)}, u32[]{:S(2)}) copy-start(f32[768]{0:T(1024)} %param.22) | copy-start | bytes 9220
  330.9 42.9 %copy-start.25 = (f32[256]{0:T(256)S(1)}, f32[256]{0:T(256)}, u32[]{:S(2)}) copy-start(f32[256]{0:T(256)} %copy-done.24) | copy-start | bytes 3076
  330.9 42.9 %copy-start.27 = (f32[256]{0:T(256)S(1)}, f32[256]{0:T(256)}, u32[]{:S(2)}) copy-start(f32[256]{0:T(256)} %copy-done.26) | copy-start | bytes 3076
  330.9 45.0 %copy-start.28 = (f32[768]{0:T(1024)S(1)}, f32[768]{0:T(1024)}, u32[]{:S(2)}) copy-start(f32[768]{0:T(1024)} %get-tuple-element.40) | copy-start | bytes 9220
  330.9 89.3 %copy-start.2 = (bf16[256,768]{1,0:T(8,128)(2,1)S(1)}, bf16[256,768]{1,0:T(8,128)(2,1)}, u32[]{:S(2)}) copy-start(bf16[256,768]{1,0:T(8,128)(2,1)} %get-tuple-element.41) | copy-start | bytes 1179652
  330.9 89.3 %copy-start.32 = (f32[768]{0:T(1024)S(1)}, f32[768]{0:T(1024)}, u32[]{:S(2)}) copy-start(f32[768]{0:T(1024)} %param.31) | copy-start | bytes 9220
  330.9 89.3 %copy-start.33 = (f32[768]{0:T(1024)S(1)}, f32[768]{0:T(1024)}, u32[]{:S(2)}) copy-start(f32[768]{0:T(1024)} %param.27) | copy-start | bytes 9220
  418.9 129.4 %copy-start.34 = (f32[768]{0:T(1024)}, f32[768]{0:T(1024)S(1)}, u32[]{:S(2)}) copy-start(f32[768]{0:T(1024)S(1)} %get-tuple-element.103) | copy-start | bytes 9220
  (24 other events, 92.3 us)
Sparse Core Ops, SparseCore 0:
  12.1 39.7 all-gather.5
  53.7 22.7 all-gather.9
  78.7 45.4 all-gather.7
  125.6 35.8 all-gather.13
  163.2 22.7 all-gather.11
  189.6 34.9 reduce-scatter.21
  226.9 79.1 reduce-scatter.13
  311.8 61.8 reduce-scatter.11
  376.1 36.0 reduce-scatter.9
  415.9 41.4 reduce-scatter.17
  461.3 42.3 reduce-scatter.19
  507.5 40.1 reduce-scatter.15
